TPU v7x, 256 devices: a whole 4x4x8 slice. The times are simulated.
256 devices in a mesh: gx: 16 (over x_lo, z), gz: 16 (over y, x_hi, core).
Axes of the slice: x: 4 (x_hi: 2, x_lo: 2; x = x_hi * 2 + x_lo), y: 4, z: 8, core: 2. Of those that a mesh axis runs over, the one named last changes fastest.
Arguments:
- conserved_fields: float32 [6, 256, 512, 128], P(None, 'gx', 'gz'), may hold values from -2 to 62, as said below
- coeff: bfloat16 [2, 1024, 6, 128, 512], P(None, 'gx', None, 'gz'), may hold values from -0.25 to 0.25
- feed_plane: int32 [25], replicated, may hold values from 0 to 2047
Outputs:
- new_state: float32 [6, 256, 512, 128], P(None, 'gx', 'gz')
Inputs may be any that keep to these rules, and one draw needn't show every extreme that they name: `conserved_fields`: each cell is the conserved form of a gas with density 0.5 to 2, temperature 0.5 to 2, streamwise velocity -1 to 7, wall-normal and spanwise velocities -1 to 1 and vibrational energy per unit mass 0.05 to 0.5.
All inputs are finite; a program needn't handle non-finite values.
Results may differ from a plain program's by a relative error of at most 0.00038.
Values sent between devices are 32-bit elements; how exact they have to be, the bound alone decides.
A program may use at most 192 MiB of HBM per device.

v0:
```python
import math
import jax
import jax.numpy as jnp
from jax import lax
from jax.sharding import PartitionSpec as P

ADIABATIC_INDEX = 1.4
CAPACITY_CONST = 2.5
OSCILLATOR_SCALE = 2.0
VIBRANT_LAG = 0.5
LANDAU_FIT_LAW = 1.5
SURFACE_DIST_SQ = 0.36
TIME_STEP = 0.05
FORCING_RATE = 2.0
WENO_EPSILON = 1e-06


def cut_along(x, dim, devices):
    before, after = (x.shape[:dim], x.shape[dim + 1 :])
    return jnp.moveaxis(x.reshape(*before, devices, -1, *after), dim, 0)


def summed_on_arrival(x, axis, dim):
    devices = lax.axis_size(axis)
    tiles = lax.all_to_all(cut_along(x, dim, devices), axis, 0, 0, tiled=True)
    return jnp.sum(tiles, axis=0)


def with_halo(x, sides, width):
    for axis, dim in sides:
        devices, length = (lax.axis_size(axis), x.shape[dim])
        up = [(i, (i + 1) % devices) for i in range(devices)]
        down = [(j, i) for i, j in up]
        last = lax.slice_in_dim(x, length - width, length, axis=dim)
        leading = lax.slice_in_dim(x, 0, width, axis=dim)
        before = lax.ppermute(last, axis, up)
        after = lax.ppermute(leading, axis, down)
        x = jnp.concatenate([before, x, after], axis=dim)
    return x


def caloric_bundle(conserved_fields):
    fluid_rho_field = conserved_fields[0]
    motion_share = (
        0.5
        * (
            jnp.square(conserved_fields[1])
            + jnp.square(conserved_fields[2])
            + jnp.square(conserved_fields[3])
        )
        / jnp.square(fluid_rho_field)
    )
    translational_kelvin = (
        conserved_fields[4] / fluid_rho_field - motion_share - conserved_fields[5] / fluid_rho_field
    ) / CAPACITY_CONST
    thermodynamic_stress = fluid_rho_field * translational_kelvin
    return (fluid_rho_field, translational_kelvin, thermodynamic_stress)


def directional(extended_fields, component):
    fluid_rho_field, translational_kelvin, thermodynamic_stress = caloric_bundle(extended_fields)
    crossflow_flux_field = extended_fields[component] / fluid_rho_field
    flux_rows = []
    for member in range(6):
        entry = extended_fields[member] * crossflow_flux_field
        if member == component:
            entry = entry + thermodynamic_stress
        if member == 4:
            entry = entry + thermodynamic_stress * crossflow_flux_field
        flux_rows.append(entry)
    forcing_samples = jnp.abs(crossflow_flux_field) + jnp.sqrt(
        ADIABATIC_INDEX * translational_kelvin
    )
    return (jnp.stack(flux_rows), forcing_samples)


def weno_face(minus_two, minus_one, centre, plus_one, plus_two):
    low_poly = (2.0 * minus_two - 7.0 * minus_one + 11.0 * centre) / 6.0
    mid_poly = (-minus_one + 5.0 * centre + 2.0 * plus_one) / 6.0
    high_poly = (2.0 * centre + 5.0 * plus_one - plus_two) / 6.0
    low_beta = 13.0 / 12.0 * jnp.square(minus_two - 2.0 * minus_one + centre) + 0.25 * jnp.square(
        minus_two - 4.0 * minus_one + 3.0 * centre
    )
    mid_beta = 13.0 / 12.0 * jnp.square(minus_one - 2.0 * centre + plus_one) + 0.25 * jnp.square(
        minus_one - plus_one
    )
    high_beta = 13.0 / 12.0 * jnp.square(centre - 2.0 * plus_one + plus_two) + 0.25 * jnp.square(
        3.0 * centre - 4.0 * plus_one + plus_two
    )
    low_weight = 0.1 / jnp.square(WENO_EPSILON + low_beta)
    mid_weight = 0.6 / jnp.square(WENO_EPSILON + mid_beta)
    high_weight = 0.3 / jnp.square(WENO_EPSILON + high_beta)
    return (low_weight * low_poly + mid_weight * mid_poly + high_weight * high_poly) / (
        low_weight + mid_weight + high_weight
    )


def sweep_axis(extended_fields, axis, component):
    length = extended_fields.shape[axis] - 6
    fluxes, forcing_samples = directional(extended_fields, component)

    def window(array, offset, dim):
        return lax.slice_in_dim(array, offset, offset + length + 1, axis=dim)

    wave_speed = window(forcing_samples, 0, axis - 1)
    for offset in range(1, 6):
        wave_speed = jnp.maximum(wave_speed, window(forcing_samples, offset, axis - 1))
    wave_speed = wave_speed[None]
    upwind = [
        0.5 * (window(fluxes, offset, axis) + wave_speed * window(extended_fields, offset, axis))
        for offset in range(5)
    ]
    downwind = [
        0.5 * (window(fluxes, offset, axis) - wave_speed * window(extended_fields, offset, axis))
        for offset in (5, 4, 3, 2, 1)
    ]
    face_flux = weno_face(*upwind) + weno_face(*downwind)
    return lax.slice_in_dim(face_flux, 1, length + 1, axis=axis) - lax.slice_in_dim(
        face_flux, 0, length, axis=axis
    )


def wall_pad(conserved_fields):
    reflected_fields = conserved_fields[:, :, :, 2::-1]
    translational_kelvin = caloric_bundle(reflected_fields)[1]
    ghost_layer_kelvin = SURFACE_DIST_SQ / translational_kelvin
    ghost_layer_oscillator = reflected_fields[4] - CAPACITY_CONST * reflected_fields[0] * (
        translational_kelvin - ghost_layer_kelvin
    )
    ghost_cells = jnp.stack(
        [
            reflected_fields[0],
            -reflected_fields[1],
            -reflected_fields[2],
            -reflected_fields[3],
            ghost_layer_oscillator,
            reflected_fields[5],
        ]
    )
    top_cells = jnp.repeat(conserved_fields[:, :, :, -1:], 3, axis=3)
    return jnp.concatenate([ghost_cells, conserved_fields, top_cells], axis=3)


def relaxation(conserved_fields):
    fluid_rho_field, translational_kelvin, thermodynamic_stress = caloric_bundle(conserved_fields)
    balanced_oscillator_share = OSCILLATOR_SCALE / (
        jnp.exp(OSCILLATOR_SCALE / translational_kelvin) - 1.0
    )
    settling_interval = (
        VIBRANT_LAG
        * jnp.exp(LANDAU_FIT_LAW * (jnp.exp(-jnp.log(translational_kelvin) / 3.0) - 1.0))
        / thermodynamic_stress
    )
    return (fluid_rho_field * balanced_oscillator_share - conserved_fields[5]) / settling_interval


def local(conserved_fields, coeff, feed_plane):
    groups_x = lax.axis_size("gx")
    groups_z = lax.axis_size("gz")
    plane_count = conserved_fields.shape[1]
    span_cells = conserved_fields.shape[2]
    span_total = span_cells * groups_z
    kx_local = coeff.shape[1]
    levels_local = coeff.shape[3]
    span_modes = coeff.shape[4]
    stream_points = 2 * kx_local * groups_x
    planes = feed_plane.shape[0]
    span_ids = (
        jnp.arange(span_modes, dtype=jnp.int32)[:, None]
        * jnp.arange(span_total, dtype=jnp.int32)[None, :]
        % span_modes
    )
    span_angle = 2.0 * math.pi / span_modes * span_ids.astype(jnp.float32)
    span_table = jnp.concatenate([jnp.cos(span_angle), jnp.sin(span_angle)], axis=1).astype(
        jnp.bfloat16
    )
    mode_ids = lax.axis_index("gx") * kx_local + jnp.arange(kx_local, dtype=jnp.int32)
    stream_ids = feed_plane[:, None] * mode_ids[None, :] % stream_points
    stream_angle = 2.0 * math.pi / stream_points * stream_ids.astype(jnp.float32)
    stream_table = jnp.concatenate([jnp.cos(stream_angle), -jnp.sin(stream_angle)], axis=1).astype(
        jnp.bfloat16
    )
    coeff_rows = coeff.reshape(2 * kx_local * 6 * levels_local, span_modes)
    product = jnp.dot(coeff_rows, span_table, preferred_element_type=jnp.float32)
    product = product.reshape(2, kx_local, 6, levels_local, 2 * span_total)
    real_part = product[0, :, :, :, :span_total] - product[1, :, :, :, span_total:]
    imag_part = product[0, :, :, :, span_total:] + product[1, :, :, :, :span_total]
    mixed_modes = jnp.concatenate([real_part, imag_part], axis=0).astype(jnp.bfloat16)
    row_block = (6 * planes + groups_x - 1) // groups_x
    total_rows = row_block * groups_x
    table_rows = total_rows // 6 + 3
    padded_table = jnp.concatenate(
        [stream_table, jnp.zeros((table_rows - planes, 2 * kx_local), jnp.bfloat16)], axis=0
    )
    modes_flat = mixed_modes.reshape(2 * kx_local, 6 * levels_local * span_total)
    start = jnp.int32(0)
    plane_span = row_block * lax.axis_size("gx") // 6 + 2
    first_plane = start // 6
    table_block = lax.dynamic_slice_in_dim(padded_table, first_plane, plane_span, 0)
    products = jnp.dot(table_block, modes_flat, preferred_element_type=jnp.float32)
    products = products.reshape(plane_span * 6, levels_local * span_total)
    reduced = summed_on_arrival(
        lax.dynamic_slice_in_dim(products, start, row_block * lax.axis_size("gx"), 0), "gx", 0
    )
    reduced = reduced.reshape(row_block, levels_local, span_total)
    relaid = lax.all_to_all(reduced, "gz", split_axis=2, concat_axis=1, tiled=True)
    collected = lax.all_gather(relaid, "gx", axis=0, tiled=True)
    feed_values = collected[: 6 * planes].reshape(planes, 6, levels_local * groups_z, span_cells)
    target = jnp.transpose(feed_values, (1, 0, 3, 2))
    stream_pad = with_halo(conserved_fields, (("gx", 1),), 3)
    span_pad = with_halo(conserved_fields, (("gz", 2),), 3)
    at_inlet = lax.axis_index("gx") == 0
    at_outlet = lax.axis_index("gx") == groups_x - 1
    lower = jnp.where(at_inlet, jnp.repeat(conserved_fields[:, :1], 3, axis=1), stream_pad[:, :3])
    upper = jnp.where(
        at_outlet, jnp.repeat(conserved_fields[:, -1:], 3, axis=1), stream_pad[:, -3:]
    )
    stream_pad = jnp.concatenate([lower, conserved_fields, upper], axis=1)
    tendency = -(
        sweep_axis(stream_pad, 1, 1)
        + sweep_axis(span_pad, 2, 3)
        + sweep_axis(wall_pad(conserved_fields), 3, 2)
    )
    tendency = tendency.at[5].add(relaxation(conserved_fields))
    plane_global = lax.axis_index("gx") * plane_count + jnp.arange(plane_count, dtype=jnp.int32)
    inside = plane_global < planes
    strength = jnp.where(
        inside, FORCING_RATE * jnp.square(1.0 - plane_global.astype(jnp.float32) / planes), 0.0
    )
    picked = jnp.take(target, jnp.minimum(plane_global, planes - 1), axis=1)
    tendency = tendency + strength[None, :, None, None] * (picked - conserved_fields)
    return conserved_fields + TIME_STEP * tendency


def solution(mesh):
    placed = (P(None, "gx", "gz", None), P(None, "gx", None, "gz", None), P())
    return jax.shard_map(
        local, mesh=mesh, in_specs=placed, out_specs=P(None, "gx", "gz", None), check_vma=False
    )
```

profile of v0, /device:TPU:8, one launch (start us, length us, event | category | flops | bytes accessed | tf_op | source)
XLA Modules:
  0.0 323.3 jit_solution(15336654425104593148)
XLA Ops:
  6.5 1.7 constant_dynamic-update-slice_fusion.1
  9.0 2.3 collective-permute-start.3
  11.4 0.9 fusion.91
  12.3 5.9 %collective-permute-start.1 = (f32[6,3,32,128]{3,2,0,1:T(8,128)}, f32[6,3,32,128]{3,2,0,1:T(8,128)}, u32[]{:S(2)}, u32[]{:S(2)}) collective-permute-start(f32[6,3,32,128]{3,2,0,1:T(8,128)} %get-tuple-element.31), channel_id=1, source_target_pairs={{16,0},{32,16},{48,32},{64,48},{80,64},{96,80},{112,96},{128,112},... | collective-permute-start | bytes 884744 | tf_op jit(solution)/shard_map/ppermute | solution.py:37
  18.2 4.9 %sine_convert_fusion = (bf16[512,512]{1,0:T(8,128)(2,1)}, bf16[512,512]{1,0:T(8,128)(2,1)}) fusion(), kind=kLoop, calls=%fused_computation.114 | loop fusion | flops 4194304 | bytes 1048576 | tf_op jit(solution)/shard_map/convert.5
  23.1 14.0 %convolution_bitcast_fusion = f32[6144,1024]{0,1:T(8,128)} fusion(bf16[6144,512]{1,0:T(8,128)(2,1)} %bitcast.56, bf16[512,512]{1,0:T(8,128)(2,1)} %get-tuple-element.44, bf16[512,512]{1,0:T(8,128)(2,1)} %get-tuple-element.45), kind=kOutput, calls=%fused_computation.1 | convolution fusion | flops 6444548096 | bytes 32505856 | tf_op jit(solution)/shard_map/dot_general | solution.py:184
  37.1 24.7 %copy.173 = f32[6144,1024]{1,0:T(8,128)} copy(f32[6144,1024]{0,1:T(8,128)} %convolution_bitcast_fusion) | data formatting | bytes 50331648 | tf_op jit(solution)/shard_map/dot_general | solution.py:184
  61.9 12.3 %fusion.1 = (bf16[1,64,6,8,512]{4,3,2,1,0:T(8,128)(2,1)}, bf16[1,64,6,8,512]{4,3,2,1,0:T(8,128)(2,1)}) fusion(f32[2,64,6,8,1024]{4,3,2,1,0:T(8,128)} %bitcast.47), kind=kLoop, calls=%fused_computation.5 | loop fusion | flops 6291456 | bytes 31457280 | tf_op jit(solution)/shard_map/convert.3
  74.1 4.8 %add.739 = bf16[64,24576]{1,0:T(8,128)(2,1)} reshape(bf16[1,64,6,8,512]{4,3,2,1,0:T(8,128)(2,1)} %get-tuple-element.27) | data formatting | bytes 6291456 | tf_op jit(solution)/shard_map/add | solution.py:187
  79.0 4.8 %sub.382 = bf16[64,24576]{1,0:T(8,128)(2,1)} reshape(bf16[1,64,6,8,512]{4,3,2,1,0:T(8,128)(2,1)} %get-tuple-element.26) | data formatting | bytes 6291456 | tf_op jit(solution)/shard_map/sub | solution.py:186
  84.0 5.6 %fusion.2 = f32[28,24576]{1,0:T(8,128)} fusion(bf16[64,24576]{1,0:T(8,128)(2,1)} %add.739, bf16[64,24576]{1,0:T(8,128)(2,1)} %sub.382, bf16[25,64]{1,0:T(8,128)(2,1)S(1)} %get-tuple-element.43, bf16[25,64]{1,0:T(8,128)(2,1)S(1)} %get-tuple-element.42), kind=kOutput, calls=%fused_computation.6 | convolution fusion | flops 188772352 | bytes 9050368 | tf_op jit(solution)/shard_map/dot_general | solution.py:200
  89.5 3.3 %reshape.160 = f32[168,4096]{1,0:T(8,128)} reshape(f32[28,24576]{1,0:T(8,128)} %fusion.2) | data formatting | bytes 5505024 | tf_op jit(solution)/shard_map/reshape | solution.py:201
  92.8 3.5 %dynamic_slice.8 = f32[160,4096]{1,0:T(8,128)} slice(f32[168,4096]{1,0:T(8,128)} %reshape.160), slice={[0:160], [0:4096]} | slice | bytes 5242880 | tf_op jit(solution)/shard_map/dynamic_slice | solution.py:203
  96.3 3.5 %reshape.161 = f32[16,10,4096]{2,1,0:T(8,128)} reshape(f32[160,4096]{1,0:T(8,128)} %dynamic_slice.8) | data formatting | bytes 5242880 | tf_op jit(solution)/shard_map/reshape | solution.py:20
  99.8 5.6 %all-to-all-start = ((f32[16,10,4096]{2,1,0:T(8,128)}), f32[16,10,4096]{2,1,0:T(8,128)}, u32[]{:S(2)}, u32[]{:S(2)}) async-start(f32[16,10,4096]{2,1,0:T(8,128)} %reshape.161), calls=%async_computation | async-start | bytes 8388608 | tf_op jit(solution)/shard_map/all_to_all | solution.py:25
  105.4 3.1 slice.508
  108.5 1.2 fusion.93
  110.4 2.8 copy.191
  113.3 1.7 copy.184
  115.0 1.3 constant_dynamic-update-slice_fusion.7
  116.3 1.7 copy.185
  118.1 1.7 copy.186
  119.8 1.7 copy.187
  121.5 1.7 copy.188
  123.2 1.7 copy.189
  125.0 1.4 constant_dynamic-update-slice_fusion.6
  126.3 1.3 constant_dynamic-update-slice_fusion.5
  127.7 1.3 constant_dynamic-update-slice_fusion.4
  129.0 1.5 constant_dynamic-update-slice_fusion.3
  130.5 1.4 constant_dynamic-update-slice_fusion.2
  131.8 2.7 copy.162
  134.5 1.4 reshape.157
  135.9 1.4 pad_maximum_fusion.2
  139.4 19.7 %divide_add_fusion = f32[6,16,32,129]{3,2,0,1:T(8,128)} fusion(f32[6,16,32,3]{3,2,0,1:T(8,128)S(1)} %reshape.157, f32[6,16,32,128]{3,2,0,1:T(8,128)S(1)} %get-tuple-element.35, f32[6,16,32,134]{3,2,0,1:T(8,128)S(1)} %multiply_dynamic-update-slice_fusion.1, f32[6,16,32,3]{3,2,0,1:T(8,128)S(1)} %copy-done.4, f32[16,32,129]{2,1,0:T(8,128)S(1)} %slice_maximum_fusion), kind=kLoop, calls=%fused_computation.33 | loop fusion | flops 60632064 | bytes 13006848 | tf_op jit(solution)/shard_map/add | solution.py:117
  159.1 1.3 pad_maximum_fusion.5
  161.2 1.0 constant_dynamic-update-slice_fusion
  162.2 13.0 %divide_add_fusion.1 = f32[6,16,33,128]{3,2,0,1:T(8,128)} fusion(f32[6,16,35,128]{3,2,0,1:T(8,128)S(1)} %constant_dynamic-update-slice_fusion, f32[6,16,38,128]{3,2,0,1:T(8,128)S(1)} %multiply_dynamic-update-slice_fusion.11, f32[6,16,32,128]{3,2,0,1:T(8,128)S(1)} %get-tuple-element.35, f32[6,16,3,128]{3,2,0,1:T(4,128)} %collective-permute-done.2, ...), kind=kLoop, calls=%fused_computation.62 | loop fusion | flops 60825600 | bytes 18210816 | tf_op jit(solution)/shard_map/add | solution.py:117
  175.3 1.0 broadcast_select_fusion
  177.6 1.1 copy-done.2
  178.7 0.8 multiply_dynamic-update-slice_fusion.9
  179.5 22.3 %all-to-all-done = f32[16,10,4096]{2,1,0:T(8,128)} async-done(((f32[16,10,4096]{2,1,0:T(8,128)}), f32[16,10,4096]{2,1,0:T(8,128)}, u32[]{:S(2)}, u32[]{:S(2)}) %all-to-all-start) | async-done | bytes 2621472 | tf_op jit(solution)/shard_map/all_to_all | solution.py:25
  201.9 2.4 reduce_sum.9
  204.5 2.0 copy.174
  206.6 4.0 %reshape.206 = f32[16,1,2560]{2,1,0:T(1,128)} reshape(f32[512,8,10]{2,1,0:T(8,128)} %bitcast.49) | data formatting | bytes 327680
  210.6 6.0 %all-to-all-start.1 = ((f32[16,1,2560]{2,1,0:T(1,128)}), f32[16,1,2560]{2,1,0:T(1,128)S(1)}, u32[]{:S(2)}, u32[]{:S(2)}) async-start(f32[16,1,2560]{2,1,0:T(1,128)} %reshape.206), calls=%async_computation.1 | async-start | bytes 327680 | tf_op jit(solution)/shard_map/all_to_all | solution.py:206
  217.4 5.6 %all-to-all-done.1 = f32[16,1,2560]{2,1,0:T(1,128)S(1)} async-done(((f32[16,1,2560]{2,1,0:T(1,128)}), f32[16,1,2560]{2,1,0:T(1,128)S(1)}, u32[]{:S(2)}, u32[]{:S(2)}) %all-to-all-start.1) | async-done | bytes 163872 | tf_op jit(solution)/shard_map/all_to_all | solution.py:206
  223.5 1.0 reduce.2
  224.6 3.6 %reshape.207 = f32[512,8,10]{2,1,0:T(8,128)} reshape(f32[16,2560]{1,0:T(8,128)S(1)} %reduce.2) | data formatting | bytes 327680
  228.1 3.3 %copy.176 = f32[10,16,8,32]{3,2,1,0:T(8,128)} copy(f32[10,16,8,32]{0,2,3,1:T(8,128)} %bitcast.50) | data formatting | bytes 327680 | tf_op jit(solution)/shard_map/all_to_all | solution.py:206
  231.5 2.0 copy.177
  233.5 2.2 add_dynamic-update-slice_fusion.1
  235.6 1.8 multiply_dynamic-update-slice_fusion.8
  237.4 0.8 multiply_dynamic-update-slice_fusion.7
  238.3 0.9 multiply_dynamic-update-slice_fusion.5
  239.2 0.8 multiply_dynamic-update-slice_fusion.6
  240.0 11.2 %divide_add_fusion.2 = f32[6,17,32,128]{3,2,0,1:T(8,128)S(1)} fusion(f32[6,3,32,128]{3,2,0,1:T(8,128)S(1)} %broadcast_select_fusion, f32[6,16,32,128]{3,2,0,1:T(8,128)S(1)} %get-tuple-element.35, f32[6,22,32,128]{3,2,0,1:T(8,128)} %multiply_dynamic-update-slice_fusion.6, f32[6,3,32,128]{3,2,0,1:T(8,128)S(1)} %copy-done.8, f32[17,32,128]{2,1,0:T(8,128)S(1)} %copy-done.9), kind=kLoop, calls=%fused_computation.87 | loop fusion | flops 63922176 | bytes 14139392 | tf_op jit(solution)/shard_map/add | solution.py:117
  251.3 1.9 fusion.47
  253.2 2.0 fusion.70
  255.2 50.4 %all-gather.2.cloned.1.call-done = f32[160,128,32]{1,2,0:T(8,128)} async-done(((f32[10,128,32]{1,2,0:T(8,128)}), f32[160,128,32]{1,2,0:T(8,128)}) %all-gather.2.cloned.1.call-update) | async-done | bytes 2621456 | tf_op jit(solution)/shard_map/all_gather | solution.py:207
  305.6 1.7 slice-done
  307.3 1.7 copy.197
  309.0 3.6 %gather_fusion = f32[16,6,32,128]{3,2,1,0:T(8,128)} fusion(f32[6,25,32,128]{3,2,1,0:T(8,128)} %bitcast.51, s32[1024]{0:T(1024)S(1)} %pad_clamp_fusion), kind=kCustom, calls=%fused_computation | custom fusion | bytes 3145792 | tf_op jit(solution)/shard_map/jit(_take)/gather | solution.py:230
  312.6 2.5 fusion.52
  315.1 1.3 copy.181
  (65 shorter events, 7.3 us)
Async XLA Ops:
  9.0 150.0 %collective-permute-start.3 = (f32[6,16,3,128]{3,2,0,1:T(4,128)}, f32[6,16,3,128]{3,2,0,1:T(4,128)}, u32[]{:S(2)}, u32[]{:S(2)}) collective-permute-start(f32[6,16,3,128]{3,2,0,1:T(4,128)} %get-tuple-element.33), channel_id=1, source_target_pairs={{1,0},{2,1},{3,2},{4,3},{5,4},{6,5},{7,6},{8,7},{9,8},{10,9},{11,1... | collective-permute-start | bytes 442376 | tf_op jit(solution)/shard_map/ppermute | solution.py:37
  11.4 147.7 %collective-permute-start.2 = (f32[6,16,3,128]{3,2,0,1:T(4,128)}, f32[6,16,3,128]{3,2,0,1:T(4,128)}, u32[]{:S(2)}, u32[]{:S(2)}) collective-permute-start(f32[6,16,3,128]{3,2,0,1:T(4,128)} %get-tuple-element.32), channel_id=1, source_target_pairs={{0,1},{1,2},{2,3},{3,4},{4,5},{5,6},{6,7},{7,8},{8,9},{9,10},{10,1... | collective-permute-start | bytes 442376 | tf_op jit(solution)/shard_map/ppermute | solution.py:36
  12.3 163.0 %collective-permute-start.1 = (f32[6,3,32,128]{3,2,0,1:T(8,128)}, f32[6,3,32,128]{3,2,0,1:T(8,128)}, u32[]{:S(2)}, u32[]{:S(2)}) collective-permute-start(f32[6,3,32,128]{3,2,0,1:T(8,128)} %get-tuple-element.31), channel_id=1, source_target_pairs={{16,0},{32,16},{48,32},{64,48},{80,64},{96,80},{112,96},{128,112},... | collective-permute-start | bytes 884744 | tf_op jit(solution)/shard_map/ppermute | solution.py:37
  18.2 158.1 %collective-permute-start = (f32[6,3,32,128]{3,2,0,1:T(8,128)}, f32[6,3,32,128]{3,2,0,1:T(8,128)}, u32[]{:S(2)}, u32[]{:S(2)}) collective-permute-start(f32[6,3,32,128]{3,2,0,1:T(8,128)} %get-tuple-element.30), channel_id=1, source_target_pairs={{0,16},{16,32},{32,48},{48,64},{64,80},{80,96},{96,112},{112,128},... | collective-permute-start | bytes 884744 | tf_op jit(solution)/shard_map/ppermute | solution.py:36
  79.0 4.8 %copy-start.12 = (s32[25]{0:T(128)S(1)}, s32[25]{0:T(128)}, u32[]{:S(2)}) copy-start(s32[25]{0:T(128)} %param.7) | copy-start | bytes 304
  99.8 102.1 %all-to-all-start = ((f32[16,10,4096]{2,1,0:T(8,128)}), f32[16,10,4096]{2,1,0:T(8,128)}, u32[]{:S(2)}, u32[]{:S(2)}) async-start(f32[16,10,4096]{2,1,0:T(8,128)} %reshape.161), calls=%async_computation | async-start | bytes 8388608 | tf_op jit(solution)/shard_map/all_to_all | solution.py:25
  105.4 3.2 copy-start
  134.5 1.4 copy-start.4
  162.2 13.0 %copy-start.11 = (f32[6,32,128]{2,1,0:T(8,128)S(1)}, f32[6,32,128]{2,1,0:T(8,128)}, u32[]{:S(2)}) copy-start(f32[6,32,128]{2,1,0:T(8,128)} %get-tuple-element.29) | copy-start | bytes 294916
  162.2 14.1 %copy-start.10 = (f32[6,32,128]{2,1,0:T(8,128)S(1)}, f32[6,32,128]{2,1,0:T(8,128)}, u32[]{:S(2)}) copy-start(f32[6,32,128]{2,1,0:T(8,128)} %get-tuple-element.28) | copy-start | bytes 294916
  176.3 0.7 copy-start.7
  177.3 1.4 copy-start.2
  210.6 12.4 %all-to-all-start.1 = ((f32[16,1,2560]{2,1,0:T(1,128)}), f32[16,1,2560]{2,1,0:T(1,128)S(1)}, u32[]{:S(2)}, u32[]{:S(2)}) async-start(f32[16,1,2560]{2,1,0:T(1,128)} %reshape.206), calls=%async_computation.1 | async-start | bytes 327680 | tf_op jit(solution)/shard_map/all_to_all | solution.py:206
  216.6 89.0 %all-gather.2.cloned.1.call-start = ((), (), s32[]{:S(2)}) async-start(), calls=%async_computation.2 | async-start | bytes 2785280 | tf_op jit(solution)/shard_map/all_gather | solution.py:207
  233.5 4.0 %copy-start.3 = (f32[6,22,32,128]{3,2,0,1:T(8,128)S(1)}, f32[6,22,32,128]{3,2,0,1:T(8,128)}, u32[]{:S(2)}) copy-start(f32[6,22,32,128]{3,2,0,1:T(8,128)} %copy-done.2) | copy-start | bytes 6488068
  237.4 2.6 copy-start.8
  237.4 2.6 copy-start.9
  240.0 11.3 %copy-start.5 = (f32[6,16,33,128]{3,2,0,1:T(8,128)S(1)}, f32[6,16,33,128]{3,2,0,1:T(8,128)}, u32[]{:S(2)}) copy-start(f32[6,16,33,128]{3,2,0,1:T(8,128)} %divide_add_fusion.1) | copy-start | bytes 4866052
  240.0 11.3 %copy-start.6 = (f32[6,16,32,129]{3,2,0,1:T(8,128)S(1)}, f32[6,16,32,129]{3,2,0,1:T(8,128)}, u32[]{:S(2)}) copy-start(f32[6,16,32,129]{3,2,0,1:T(8,128)} %divide_add_fusion) | copy-start | bytes 4755460
  305.6 1.7 slice-start
  309.0 3.6 %copy-start.1 = (f32[6,16,32,128]{3,2,1,0:T(8,128)S(1)}, f32[6,16,32,128]{3,2,1,0:T(8,128)}, u32[]{:S(2)}) copy-start(f32[6,16,32,128]{3,2,1,0:T(8,128)} %param.5) | copy-start | bytes 4718596
Sparse Core Ops, SparseCore 0:
  233.6 71.9 all-gather.1
where the time goes:
time: 325 us; the launch traced here: 323 us
  local copies, waits for them, and re-layouts  99.8 us (31%)
  other arithmetic  91.9 us (28%)
  waiting for transfers between devices  78.4 us (24%)
  starting transfers between devices  19.9 us (6%)
  matrix products  19.6 us (6%)
  between operations  13.7 us (4%)
    all_gather x1, waiting for transfers between devices, local(): collected = lax.all_gather(relaid, 'gx', axis=0, tiled=True)  50.4 us
    add x3, other arithmetic, sweep_axis(): face_flux = weno_face(*upwind) + weno_face(*downwind)  44 us
    dot_general x1, local copies, waits for them, and re-layouts, local(): jnp.dot(coeff_rows, span_table, preferred_element_type=jnp.float32)  24.7 us
    unnamed x37, local copies, waits for them, and re-layouts  23 us
    all_to_all x1, waiting for transfers between devices, summed_on_arrival(): tiles = lax.all_to_all(cut_along(x, dim, devices), axis, 0, 0, tiled=True)  22.3 us
    another operation x3, other arithmetic  17.4 us
    dot_general x1, matrix products, local(): jnp.dot(coeff_rows, span_table, preferred_element_type=jnp.float32)  14 us
    unnamed x19, other arithmetic  13 us
  transfers between devices with their start and end apart: 7, of which 3 were waited for; matrix products, arithmetic and copies ran while one was open for 55% of the time, Pallas kernels for 0%

commit v1 on v0

--- a/solution.py
+++ b/solution.py
@@ -204,7 +204,9 @@
     )
     reduced = reduced.reshape(row_block, levels_local, span_total)
     relaid = lax.all_to_all(reduced, "gz", split_axis=2, concat_axis=1, tiled=True)
-    collected = lax.all_gather(relaid, "gx", axis=0, tiled=True)
+    collected = jnp.concatenate(
+        lax.all_to_all(jnp.stack([relaid] * lax.axis_size("gx")), "gx", 0, 0), axis=0
+    )
     feed_values = collected[: 6 * planes].reshape(planes, 6, levels_local * groups_z, span_cells)
     target = jnp.transpose(feed_values, (1, 0, 3, 2))
     stream_pad = with_halo(conserved_fields, (("gx", 1),), 3)

time: 325 us -> 313 us (0.963); the launches traced: 323 us -> 308 us
  between operations: 13.7 us -> 0.36 us
  waiting for transfers between devices: 78.4 us -> 66 us
  starting transfers between devices: 19.9 us -> 28 us
    all_gather x1 -> x0, waiting for transfers between devices: 50.4 us -> none  [local(): collected = lax.all_gather(relaid, 'gx', axis=0, tiled=True)]
    all_to_all x0 -> x1, waiting for transfers between devices: none -> 38.1 us  [local(): lax.all_to_all(jnp.stack([relaid] * lax.axis_size('gx')), 'gx', 0, 0)]
    all_to_all x0 -> x1, starting transfers between devices: none -> 8.2 us  [local(): lax.all_to_all(jnp.stack([relaid] * lax.axis_size('gx')), 'gx', 0, 0)]
  transfers between devices with their start and end apart: 7 -> 7, of which waited for: 3 -> 3; matrix products, arithmetic and copies ran while one was open for 55% -> 58% of each run, Pallas kernels for 0% -> 0%
where the time goes in v1:
time: 313 us; the launch traced here: 308 us
  local copies, waits for them, and re-layouts  101 us (32%)
  other arithmetic  92.3 us (29%)
  waiting for transfers between devices  66 us (21%)
  starting transfers between devices  28 us (9%)
  matrix products  19.6 us (6%)
    add x3, other arithmetic, sweep_axis(): face_flux = weno_face(*upwind) + weno_face(*downwind)  44.5 us
    all_to_all x1, waiting for transfers between devices, local(): lax.all_to_all(jnp.stack([relaid] * lax.axis_size('gx')), 'gx', 0, 0)  38.1 us
    dot_general x1, local copies, waits for them, and re-layouts, local(): jnp.dot(coeff_rows, span_table, preferred_element_type=jnp.float32)  24.8 us
    unnamed x37, local copies, waits for them, and re-layouts  23 us
    all_to_all x1, waiting for transfers between devices, summed_on_arrival(): tiles = lax.all_to_all(cut_along(x, dim, devices), axis, 0, 0, tiled=True)  22.3 us
    another operation x3, other arithmetic  17.3 us
    dot_general x1, matrix products, local(): jnp.dot(coeff_rows, span_table, preferred_element_type=jnp.float32)  14 us
    unnamed x19, other arithmetic  12.9 us
  transfers between devices with their start and end apart: 7, of which 3 were waited for; matrix products, arithmetic and copies ran while one was open for 58% of the time, Pallas kernels for 0%

profile of v1, /device:TPU:8, one launch (start us, length us, event | category | flops | bytes accessed | tf_op | source)
XLA Modules:
  0.0 307.7 jit_solution(5888211737631620050)
XLA Ops:
  0.0 1.7 constant_dynamic-update-slice_fusion.1
  1.7 0.8 fusion.92
  2.5 2.3 collective-permute-start.3
  4.9 0.9 fusion.91
  5.8 5.9 %collective-permute-start.1 = (f32[6,3,32,128]{3,2,0,1:T(8,128)}, f32[6,3,32,128]{3,2,0,1:T(8,128)}, u32[]{:S(2)}, u32[]{:S(2)}) collective-permute-start(f32[6,3,32,128]{3,2,0,1:T(8,128)} %get-tuple-element.31), channel_id=1, source_target_pairs={{16,0},{32,16},{48,32},{64,48},{80,64},{96,80},{112,96},{128,112},... | collective-permute-start | bytes 884744 | tf_op jit(solution)/shard_map/ppermute | solution.py:37
  11.7 4.9 %sine_convert_fusion = (bf16[512,512]{1,0:T(8,128)(2,1)}, bf16[512,512]{1,0:T(8,128)(2,1)}) fusion(), kind=kLoop, calls=%fused_computation.114 | loop fusion | flops 4194304 | bytes 1048576 | tf_op jit(solution)/shard_map/convert.5
  16.6 14.0 %convolution_bitcast_fusion = f32[6144,1024]{0,1:T(8,128)} fusion(bf16[6144,512]{1,0:T(8,128)(2,1)} %bitcast.56, bf16[512,512]{1,0:T(8,128)(2,1)} %get-tuple-element.44, bf16[512,512]{1,0:T(8,128)(2,1)} %get-tuple-element.45), kind=kOutput, calls=%fused_computation.1 | convolution fusion | flops 6444548096 | bytes 32505856 | tf_op jit(solution)/shard_map/dot_general | solution.py:184
  30.6 24.8 %copy.173 = f32[6144,1024]{1,0:T(8,128)} copy(f32[6144,1024]{0,1:T(8,128)} %convolution_bitcast_fusion) | data formatting | bytes 50331648 | tf_op jit(solution)/shard_map/dot_general | solution.py:184
  55.3 12.2 %fusion.1 = (bf16[1,64,6,8,512]{4,3,2,1,0:T(8,128)(2,1)}, bf16[1,64,6,8,512]{4,3,2,1,0:T(8,128)(2,1)}) fusion(f32[2,64,6,8,1024]{4,3,2,1,0:T(8,128)} %bitcast.47), kind=kLoop, calls=%fused_computation.5 | loop fusion | flops 6291456 | bytes 31457280 | tf_op jit(solution)/shard_map/convert.3
  67.6 4.8 %add.739 = bf16[64,24576]{1,0:T(8,128)(2,1)} reshape(bf16[1,64,6,8,512]{4,3,2,1,0:T(8,128)(2,1)} %get-tuple-element.27) | data formatting | bytes 6291456 | tf_op jit(solution)/shard_map/add | solution.py:187
  72.4 4.8 %sub.382 = bf16[64,24576]{1,0:T(8,128)(2,1)} reshape(bf16[1,64,6,8,512]{4,3,2,1,0:T(8,128)(2,1)} %get-tuple-element.26) | data formatting | bytes 6291456 | tf_op jit(solution)/shard_map/sub | solution.py:186
  77.4 5.6 %fusion.2 = f32[28,24576]{1,0:T(8,128)} fusion(bf16[64,24576]{1,0:T(8,128)(2,1)} %add.739, bf16[64,24576]{1,0:T(8,128)(2,1)} %sub.382, bf16[25,64]{1,0:T(8,128)(2,1)S(1)} %get-tuple-element.43, bf16[25,64]{1,0:T(8,128)(2,1)S(1)} %get-tuple-element.42), kind=kOutput, calls=%fused_computation.6 | convolution fusion | flops 188772352 | bytes 9050368 | tf_op jit(solution)/shard_map/dot_general | solution.py:200
  83.0 3.3 %reshape.166 = f32[168,4096]{1,0:T(8,128)} reshape(f32[28,24576]{1,0:T(8,128)} %fusion.2) | data formatting | bytes 5505024 | tf_op jit(solution)/shard_map/reshape | solution.py:201
  86.2 3.5 %dynamic_slice.8 = f32[160,4096]{1,0:T(8,128)} slice(f32[168,4096]{1,0:T(8,128)} %reshape.166), slice={[0:160], [0:4096]} | slice | bytes 5242880 | tf_op jit(solution)/shard_map/dynamic_slice | solution.py:203
  89.8 3.4 %reshape.167 = f32[16,10,4096]{2,1,0:T(8,128)} reshape(f32[160,4096]{1,0:T(8,128)} %dynamic_slice.8) | data formatting | bytes 5242880 | tf_op jit(solution)/shard_map/reshape | solution.py:20
  93.2 5.6 %all-to-all-start = ((f32[16,10,4096]{2,1,0:T(8,128)}), f32[16,10,4096]{2,1,0:T(8,128)}, u32[]{:S(2)}, u32[]{:S(2)}) async-start(f32[16,10,4096]{2,1,0:T(8,128)} %reshape.167), calls=%async_computation | async-start | bytes 8388608 | tf_op jit(solution)/shard_map/all_to_all | solution.py:25
  98.8 3.1 %slice.509 = f32[6,16,32,1]{3,2,1,0:T(8,128)} slice(f32[6,16,32,128]{3,2,1,0:T(8,128)} %param.5), slice={[0:6], [0:16], [0:32], [127:128]} | slice | bytes 24576 | tf_op jit(solution)/shard_map/slice | solution.py:140
  101.9 1.2 fusion.93
  103.9 2.8 copy.191
  106.7 1.7 copy.184
  108.4 1.3 constant_dynamic-update-slice_fusion.7
  109.8 1.7 copy.185
  111.5 1.7 copy.186
  113.2 1.7 copy.187
  114.9 1.7 copy.188
  116.7 1.7 copy.189
  118.4 1.3 constant_dynamic-update-slice_fusion.6
  119.7 1.3 constant_dynamic-update-slice_fusion.5
  121.1 1.4 constant_dynamic-update-slice_fusion.4
  122.4 1.5 constant_dynamic-update-slice_fusion.3
  123.9 1.3 constant_dynamic-update-slice_fusion.2
  125.2 2.7 copy.162
  127.9 1.4 reshape.163
  129.3 1.4 pad_maximum_fusion.2
  132.8 19.7 %divide_add_fusion = f32[6,16,32,129]{3,2,0,1:T(8,128)} fusion(f32[6,16,32,3]{3,2,0,1:T(8,128)S(1)} %reshape.163, f32[6,16,32,128]{3,2,0,1:T(8,128)S(1)} %get-tuple-element.35, f32[6,16,32,134]{3,2,0,1:T(8,128)S(1)} %multiply_dynamic-update-slice_fusion.1, f32[6,16,32,3]{3,2,0,1:T(8,128)S(1)} %copy-done.4, f32[16,32,129]{2,1,0:T(8,128)S(1)} %slice_maximum_fusion), kind=kLoop, calls=%fused_computation.33 | loop fusion | flops 60632064 | bytes 13006848 | tf_op jit(solution)/shard_map/add | solution.py:117
  152.5 1.3 pad_maximum_fusion.5
  154.6 1.0 constant_dynamic-update-slice_fusion
  155.6 13.1 %divide_add_fusion.1 = f32[6,16,33,128]{3,2,0,1:T(8,128)} fusion(f32[6,16,35,128]{3,2,0,1:T(8,128)S(1)} %constant_dynamic-update-slice_fusion, f32[6,16,38,128]{3,2,0,1:T(8,128)S(1)} %multiply_dynamic-update-slice_fusion.11, f32[6,16,32,128]{3,2,0,1:T(8,128)S(1)} %get-tuple-element.35, f32[6,16,3,128]{3,2,0,1:T(4,128)} %collective-permute-done.2, ...), kind=kLoop, calls=%fused_computation.62 | loop fusion | flops 60825600 | bytes 18210816 | tf_op jit(solution)/shard_map/add | solution.py:117
  168.7 1.0 broadcast_select_fusion
  171.1 1.1 copy-done.2
  173.0 22.3 %all-to-all-done = f32[16,10,4096]{2,1,0:T(8,128)} async-done(((f32[16,10,4096]{2,1,0:T(8,128)}), f32[16,10,4096]{2,1,0:T(8,128)}, u32[]{:S(2)}, u32[]{:S(2)}) %all-to-all-start) | async-done | bytes 2621472 | tf_op jit(solution)/shard_map/all_to_all | solution.py:25
  195.3 2.4 reduce_sum.9
  197.9 2.0 copy.174
  200.0 4.0 %reshape.212 = f32[16,1,2560]{2,1,0:T(1,128)} reshape(f32[512,8,10]{2,1,0:T(8,128)} %bitcast.49) | data formatting | bytes 327680
  204.0 6.0 %all-to-all-start.1 = ((f32[16,1,2560]{2,1,0:T(1,128)}), f32[16,1,2560]{2,1,0:T(1,128)S(1)}, u32[]{:S(2)}, u32[]{:S(2)}) async-start(f32[16,1,2560]{2,1,0:T(1,128)} %reshape.212), calls=%async_computation.1 | async-start | bytes 327680 | tf_op jit(solution)/shard_map/all_to_all | solution.py:206
  210.8 5.7 %all-to-all-done.1 = f32[16,1,2560]{2,1,0:T(1,128)S(1)} async-done(((f32[16,1,2560]{2,1,0:T(1,128)}), f32[16,1,2560]{2,1,0:T(1,128)S(1)}, u32[]{:S(2)}, u32[]{:S(2)}) %all-to-all-start.1) | async-done | bytes 163872 | tf_op jit(solution)/shard_map/all_to_all | solution.py:206
  216.9 1.0 reduce.2
  218.0 3.6 %reshape.213 = f32[512,8,10]{2,1,0:T(8,128)} reshape(f32[16,2560]{1,0:T(8,128)S(1)} %reduce.2) | data formatting | bytes 327680
  221.5 3.3 %copy.176 = f32[10,16,8,32]{3,2,1,0:T(8,128)} copy(f32[10,16,8,32]{0,2,3,1:T(8,128)} %bitcast.50) | data formatting | bytes 327680 | tf_op jit(solution)/shard_map/all_to_all | solution.py:206
  224.9 1.3 copy.177
  226.2 1.9 stack.17
  228.1 8.2 %all-to-all-start.2 = ((f32[16,10,128,32]{2,3,1,0:T(8,128)}), f32[16,10,128,32]{2,3,1,0:T(8,128)}, u32[]{:S(2)}, u32[]{:S(2)}) async-start(f32[16,10,128,32]{2,3,1,0:T(8,128)} %stack.17), calls=%async_computation.2 | async-start | bytes 5242880 | tf_op jit(solution)/shard_map/all_to_all | solution.py:208
  236.3 2.2 add_dynamic-update-slice_fusion.1
  238.5 1.8 multiply_dynamic-update-slice_fusion.8
  241.1 0.9 multiply_dynamic-update-slice_fusion.5
  242.8 11.7 %divide_add_fusion.2 = f32[6,17,32,128]{3,2,0,1:T(8,128)S(1)} fusion(f32[6,3,32,128]{3,2,0,1:T(8,128)S(1)} %broadcast_select_fusion, f32[6,16,32,128]{3,2,0,1:T(8,128)S(1)} %get-tuple-element.35, f32[6,22,32,128]{3,2,0,1:T(8,128)} %multiply_dynamic-update-slice_fusion.6, f32[6,3,32,128]{3,2,0,1:T(8,128)S(1)} %copy-done.8, f32[17,32,128]{2,1,0:T(8,128)S(1)} %copy-done.9), kind=kLoop, calls=%fused_computation.87 | loop fusion | flops 63922176 | bytes 14139392 | tf_op jit(solution)/shard_map/add | solution.py:117
  254.6 1.9 fusion.47
  256.4 2.0 fusion.70
  258.5 38.1 %all-to-all-done.2 = f32[16,10,128,32]{2,3,1,0:T(8,128)} async-done(((f32[16,10,128,32]{2,3,1,0:T(8,128)}), f32[16,10,128,32]{2,3,1,0:T(8,128)}, u32[]{:S(2)}, u32[]{:S(2)}) %all-to-all-start.2) | async-done | bytes 2621472 | tf_op jit(solution)/shard_map/all_to_all | solution.py:208
  296.5 2.0 slice.655
  298.5 1.7 copy.197
  300.2 3.6 %gather_fusion = f32[16,6,32,128]{3,2,1,0:T(8,128)} fusion(f32[6,25,32,128]{3,2,1,0:T(8,128)} %bitcast.51, s32[1024]{0:T(1024)S(1)} %pad_clamp_fusion), kind=kCustom, calls=%fused_computation | custom fusion | bytes 3145792 | tf_op jit(solution)/shard_map/jit(_take)/gather | solution.py:232
  303.9 2.5 fusion.52
  306.4 1.3 copy.181
  (64 shorter events, 8.9 us)
Async XLA Ops:
  2.5 149.9 %collective-permute-start.3 = (f32[6,16,3,128]{3,2,0,1:T(4,128)}, f32[6,16,3,128]{3,2,0,1:T(4,128)}, u32[]{:S(2)}, u32[]{:S(2)}) collective-permute-start(f32[6,16,3,128]{3,2,0,1:T(4,128)} %get-tuple-element.33), channel_id=1, source_target_pairs={{1,0},{2,1},{3,2},{4,3},{5,4},{6,5},{7,6},{8,7},{9,8},{10,9},{11,1... | collective-permute-start | bytes 442376 | tf_op jit(solution)/shard_map/ppermute | solution.py:37
  4.9 147.6 %collective-permute-start.2 = (f32[6,16,3,128]{3,2,0,1:T(4,128)}, f32[6,16,3,128]{3,2,0,1:T(4,128)}, u32[]{:S(2)}, u32[]{:S(2)}) collective-permute-start(f32[6,16,3,128]{3,2,0,1:T(4,128)} %get-tuple-element.32), channel_id=1, source_target_pairs={{0,1},{1,2},{2,3},{3,4},{4,5},{5,6},{6,7},{7,8},{8,9},{9,10},{10,1... | collective-permute-start | bytes 442376 | tf_op jit(solution)/shard_map/ppermute | solution.py:36
  5.8 162.9 %collective-permute-start.1 = (f32[6,3,32,128]{3,2,0,1:T(8,128)}, f32[6,3,32,128]{3,2,0,1:T(8,128)}, u32[]{:S(2)}, u32[]{:S(2)}) collective-permute-start(f32[6,3,32,128]{3,2,0,1:T(8,128)} %get-tuple-element.31), channel_id=1, source_target_pairs={{16,0},{32,16},{48,32},{64,48},{80,64},{96,80},{112,96},{128,112},... | collective-permute-start | bytes 884744 | tf_op jit(solution)/shard_map/ppermute | solution.py:37
  11.7 158.1 %collective-permute-start = (f32[6,3,32,128]{3,2,0,1:T(8,128)}, f32[6,3,32,128]{3,2,0,1:T(8,128)}, u32[]{:S(2)}, u32[]{:S(2)}) collective-permute-start(f32[6,3,32,128]{3,2,0,1:T(8,128)} %get-tuple-element.30), channel_id=1, source_target_pairs={{0,16},{16,32},{32,48},{48,64},{64,80},{80,96},{96,112},{112,128},... | collective-permute-start | bytes 884744 | tf_op jit(solution)/shard_map/ppermute | solution.py:36
  72.4 4.8 %copy-start.12 = (s32[25]{0:T(128)S(1)}, s32[25]{0:T(128)}, u32[]{:S(2)}) copy-start(s32[25]{0:T(128)} %param.7) | copy-start | bytes 304
  93.2 102.1 %all-to-all-start = ((f32[16,10,4096]{2,1,0:T(8,128)}), f32[16,10,4096]{2,1,0:T(8,128)}, u32[]{:S(2)}, u32[]{:S(2)}) async-start(f32[16,10,4096]{2,1,0:T(8,128)} %reshape.167), calls=%async_computation | async-start | bytes 8388608 | tf_op jit(solution)/shard_map/all_to_all | solution.py:25
  98.8 3.2 %copy-start = (f32[6,16,32,128]{3,2,1,0:T(8,128)S(1)}, f32[6,16,32,128]{3,2,1,0:T(8,128)}, u32[]{:S(2)}) copy-start(f32[6,16,32,128]{3,2,1,0:T(8,128)} %param.5) | copy-start | bytes 4718596
  127.9 1.4 copy-start.4
  155.6 13.1 %copy-start.11 = (f32[6,32,128]{2,1,0:T(8,128)S(1)}, f32[6,32,128]{2,1,0:T(8,128)}, u32[]{:S(2)}) copy-start(f32[6,32,128]{2,1,0:T(8,128)} %get-tuple-element.29) | copy-start | bytes 294916
  155.6 14.1 %copy-start.10 = (f32[6,32,128]{2,1,0:T(8,128)S(1)}, f32[6,32,128]{2,1,0:T(8,128)}, u32[]{:S(2)}) copy-start(f32[6,32,128]{2,1,0:T(8,128)} %get-tuple-element.28) | copy-start | bytes 294916
  169.8 0.7 copy-start.7
  170.7 1.4 copy-start.2
  204.0 12.4 %all-to-all-start.1 = ((f32[16,1,2560]{2,1,0:T(1,128)}), f32[16,1,2560]{2,1,0:T(1,128)S(1)}, u32[]{:S(2)}, u32[]{:S(2)}) async-start(f32[16,1,2560]{2,1,0:T(1,128)} %reshape.212), calls=%async_computation.1 | async-start | bytes 327680 | tf_op jit(solution)/shard_map/all_to_all | solution.py:206
  228.1 68.5 %all-to-all-start.2 = ((f32[16,10,128,32]{2,3,1,0:T(8,128)}), f32[16,10,128,32]{2,3,1,0:T(8,128)}, u32[]{:S(2)}, u32[]{:S(2)}) async-start(f32[16,10,128,32]{2,3,1,0:T(8,128)} %stack.17), calls=%async_computation.2 | async-start | bytes 5242880 | tf_op jit(solution)/shard_map/all_to_all | solution.py:208
  236.3 4.0 %copy-start.3 = (f32[6,22,32,128]{3,2,0,1:T(8,128)S(1)}, f32[6,22,32,128]{3,2,0,1:T(8,128)}, u32[]{:S(2)}) copy-start(f32[6,22,32,128]{3,2,0,1:T(8,128)} %copy-done.2) | copy-start | bytes 6488068
  240.3 2.6 copy-start.8
  240.3 2.6 copy-start.9
  242.8 11.7 %copy-start.5 = (f32[6,16,33,128]{3,2,0,1:T(8,128)S(1)}, f32[6,16,33,128]{3,2,0,1:T(8,128)}, u32[]{:S(2)}) copy-start(f32[6,16,33,128]{3,2,0,1:T(8,128)} %divide_add_fusion.1) | copy-start | bytes 4866052
  242.8 11.8 %copy-start.6 = (f32[6,16,32,129]{3,2,0,1:T(8,128)S(1)}, f32[6,16,32,129]{3,2,0,1:T(8,128)}, u32[]{:S(2)}) copy-start(f32[6,16,32,129]{3,2,0,1:T(8,128)} %divide_add_fusion) | copy-start | bytes 4755460
  300.2 3.6 %copy-start.1 = (f32[6,16,32,128]{3,2,1,0:T(8,128)S(1)}, f32[6,16,32,128]{3,2,1,0:T(8,128)}, u32[]{:S(2)}) copy-start(f32[6,16,32,128]{3,2,1,0:T(8,128)} %param.5) | copy-start | bytes 4718596
